TPU v7x, 32 devices: a whole 2x2x4 slice. The times are simulated.
32 devices in a mesh: row: 4 (over y, x), col: 8 (over z, core).
Axes of the slice: x: 2, y: 2, z: 4, core: 2. Of those that a mesh axis runs over, the one named last changes fastest.
Arguments:
- homolog_stack: bfloat16 [128, 128, 256], P(('row', 'col')), may hold values from -6 to 6
- per_amino_features: bfloat16 [128, 256], P(('row', 'col')), may hold values from -6 to 6
- asking_matrix: bfloat16 [256, 256], replicated, may hold values from -24 to 24
- lookup_matrix: bfloat16 [256, 256], replicated, may hold values from -0.375 to 0.375
- content_matrix: bfloat16 [256, 256], replicated, may hold values from -0.375 to 0.375
- sigmoid_scaling_matrix: bfloat16 [256, 256], replicated, may hold values from -0.375 to 0.375
- attention_result_matrix: bfloat16 [256, 256], replicated, may hold values from -0.375 to 0.375
- stack_transition_expand_matrix: bfloat16 [256, 1024], replicated, may hold values from -0.375 to 0.375
- stack_transition_shrink_matrix: bfloat16 [1024, 256], replicated, may hold values from -0.1875 to 0.1875
- former_factor_matrix: bfloat16 [256, 32], replicated, may hold values from -0.375 to 0.375
- latter_factor_matrix: bfloat16 [256, 32], replicated, may hold values from -0.375 to 0.375
- factor_mean_projection: bfloat16 [1024, 128], replicated, may hold values from -1.1953125 to 1.1953125
- row_amino_embedding: bfloat16 [256, 128], replicated, may hold values from -0.375 to 0.375
- column_amino_embedding: bfloat16 [256, 128], replicated, may hold values from -0.375 to 0.375
- offset_embedding_matrix: bfloat16 [65, 128], replicated, may hold values from -3 to 3
- grid_transition_expand: bfloat16 [128, 512], replicated, may hold values from -0.5 to 0.5
- grid_transition_shrink: bfloat16 [512, 128], replicated, may hold values from -0.25 to 0.25
- distance_bins_matrix: bfloat16 [128, 64], replicated, may hold values from -0.5 to 0.5
Outputs:
- alignment_output: bfloat16 [128, 128, 256], P(None, ('row', 'col'))
- pair_output: bfloat16 [128, 128, 128], P('row', 'col')
- distogram: bfloat16 [128, 128, 64], P('row', 'col')
All inputs are finite; a program needn't handle non-finite values.
Results may differ from a plain program's by a relative error of at most 0.011.
The roundings to bfloat16 on the way count: a program that leaves them out, or rounds other values in their place, can miss the bound.
Values may be sent and summed in bfloat16 or wider, within the bound.
No kernel may reach another device: no remote copies, remote signals or barrier semaphores. Data moves between devices by JAX's collectives and lax.ppermute only.
A program may use at most 256 MiB of HBM per device.

v0:
```python
import math
import jax
import jax.numpy as jnp
from jax import lax
from jax.sharding import PartitionSpec as P

HEADS = 8
HEAD = 32
CLIP = 32


def spread_2(block, axis, source):
    block = jnp.where(lax.axis_index(axis) == source, block, jnp.zeros_like(block))
    return lax.psum(block, axis)


def standardize_features(values):
    middle = jnp.mean(values, -1, keepdims=True)
    centred = values - middle
    spread = jnp.mean(centred * centred, -1, keepdims=True)
    return centred * lax.rsqrt(spread + 1e-05)


def alignment_layer(
    block_piece,
    asking_matrix,
    lookup_matrix,
    content_matrix,
    sigmoid_scaling_matrix,
    attention_result_matrix,
    stack_transition_expand_matrix,
    stack_transition_shrink_matrix,
):
    count_seq, count_res, feature_width = block_piece.shape
    start = block_piece.astype(jnp.float32).reshape(-1, feature_width)
    standardized = standardize_features(start).astype(jnp.bfloat16)
    query = jnp.dot(standardized, asking_matrix, preferred_element_type=jnp.float32).astype(
        jnp.bfloat16
    )
    key_rows = jnp.dot(standardized, lookup_matrix, preferred_element_type=jnp.float32).astype(
        jnp.bfloat16
    )
    value_rows = jnp.dot(standardized, content_matrix, preferred_element_type=jnp.float32).astype(
        jnp.bfloat16
    )
    gate = jax.nn.sigmoid(
        jnp.dot(standardized, sigmoid_scaling_matrix, preferred_element_type=jnp.float32)
    )
    query = query.reshape(count_seq, count_res, HEADS, HEAD)
    key_rows = key_rows.reshape(count_seq, count_res, HEADS, HEAD)
    value_rows = value_rows.reshape(count_seq, count_res, HEADS, HEAD)
    scores = jnp.einsum(
        "sihd,tihd->ihst", query, key_rows, preferred_element_type=jnp.float32
    ) / math.sqrt(HEAD)
    weights = jax.nn.softmax(scores, -1).astype(jnp.bfloat16)
    attended = jnp.einsum(
        "ihst,tihd->sihd", weights, value_rows, preferred_element_type=jnp.float32
    ).reshape(-1, feature_width)
    mixed = (attended * gate).astype(jnp.bfloat16)
    first_part = start + jnp.dot(mixed, attention_result_matrix, preferred_element_type=jnp.float32)
    hidden_units = jax.nn.relu(
        jnp.dot(
            standardize_features(first_part).astype(jnp.bfloat16),
            stack_transition_expand_matrix,
            preferred_element_type=jnp.float32,
        )
    ).astype(jnp.bfloat16)
    second_part = first_part + jnp.dot(
        hidden_units, stack_transition_shrink_matrix, preferred_element_type=jnp.float32
    )
    return second_part.reshape(count_seq, count_res, feature_width)


def pair_block(
    a_u,
    b_v,
    left_u,
    right_v,
    start_u,
    start_v,
    offset_embedding_matrix,
    factor_mean_projection,
    grid_transition_expand,
    grid_transition_shrink,
    distance_bins_matrix,
):
    count_seq, count_u, factor = a_u.shape
    count_v = b_v.shape[1]
    feature_width = left_u.shape[1]
    step_rows = max(1, min(count_u, 1024 // count_v))
    tile_collection = count_u // step_rows
    a_blocks = a_u.reshape(count_seq, tile_collection, step_rows, factor).transpose(1, 0, 2, 3)
    left_blocks = left_u.reshape(tile_collection, step_rows, feature_width)
    flat_v = b_v.reshape(count_seq, count_v * factor)
    columns = start_v + jnp.arange(count_v, dtype=jnp.int32)
    bins = jnp.arange(2 * CLIP + 1, dtype=jnp.int32)

    def one_block(inputs):
        a_blk, left_blk, index = inputs
        outer = lax.dot_general(
            a_blk.reshape(count_seq, step_rows * factor),
            flat_v,
            (((0,), (0,)), ((), ())),
            preferred_element_type=jnp.float32,
        )
        outer = (
            outer.reshape(step_rows, factor, count_v, factor)
            .transpose(0, 2, 1, 3)
            .reshape(step_rows * count_v, factor * factor)
        )
        outer = (outer / count_seq).astype(jnp.bfloat16)
        projected = jnp.dot(outer, factor_mean_projection, preferred_element_type=jnp.float32)
        rows_here = start_u + index * step_rows + jnp.arange(step_rows, dtype=jnp.int32)
        offset = jnp.clip(columns[None, :] - rows_here[:, None], -CLIP, CLIP) + CLIP
        onehot = (offset[:, :, None] == bins).astype(jnp.bfloat16).reshape(-1, 2 * CLIP + 1)
        relative = jnp.dot(onehot, offset_embedding_matrix, preferred_element_type=jnp.float32)
        embedded = (
            left_blk.astype(jnp.float32)[:, None, :] + right_v.astype(jnp.float32)[None, :, :]
        ).reshape(-1, feature_width)
        start_pair = embedded + relative + projected
        hidden_units = jax.nn.relu(
            jnp.dot(
                standardize_features(start_pair).astype(jnp.bfloat16),
                grid_transition_expand,
                preferred_element_type=jnp.float32,
            )
        ).astype(jnp.bfloat16)
        final = start_pair + jnp.dot(
            hidden_units, grid_transition_shrink, preferred_element_type=jnp.float32
        )
        rounded = final.astype(jnp.bfloat16)
        logits = jnp.dot(rounded, distance_bins_matrix, preferred_element_type=jnp.float32)
        return (
            rounded.reshape(step_rows, count_v, feature_width),
            logits.reshape(step_rows, count_v, -1),
        )

    pairs, logits = lax.map(
        one_block, (a_blocks, left_blocks, jnp.arange(tile_collection, dtype=jnp.int32))
    )
    return (pairs.reshape(count_u, count_v, feature_width), logits.reshape(count_u, count_v, -1))


def shards(
    homolog_stack,
    per_amino_features,
    asking_matrix,
    lookup_matrix,
    content_matrix,
    sigmoid_scaling_matrix,
    attention_result_matrix,
    stack_transition_expand_matrix,
    stack_transition_shrink_matrix,
    former_factor_matrix,
    latter_factor_matrix,
    factor_mean_projection,
    row_amino_embedding,
    column_amino_embedding,
    offset_embedding_matrix,
    grid_transition_expand,
    grid_transition_shrink,
    distance_bins_matrix,
):
    row_count = lax.axis_size("row")
    col_count = lax.axis_size("col")
    whole_mesh_axes = row_count * col_count
    homolog_shard_here, amino_collection, feature_width = homolog_stack.shape
    amino_shard_here = amino_collection // whole_mesh_axes
    fragment_collection = homolog_stack.reshape(
        1, homolog_shard_here, whole_mesh_axes, amino_shard_here, feature_width
    )
    moved = lax.all_to_all(
        fragment_collection, ("row", "col"), split_axis=2, concat_axis=0, tiled=True
    )
    local_part = moved.reshape(-1, amino_shard_here, feature_width)
    count_seq = local_part.shape[0]
    refreshed_stack = alignment_layer(
        local_part,
        asking_matrix,
        lookup_matrix,
        content_matrix,
        sigmoid_scaling_matrix,
        attention_result_matrix,
        stack_transition_expand_matrix,
        stack_transition_shrink_matrix,
    )
    alignment_output = refreshed_stack.astype(jnp.bfloat16)
    standardized = (
        standardize_features(refreshed_stack).astype(jnp.bfloat16).reshape(-1, feature_width)
    )
    left_opm = (
        jnp.dot(standardized, former_factor_matrix, preferred_element_type=jnp.float32)
        .astype(jnp.bfloat16)
        .reshape(count_seq, amino_shard_here, -1)
    )
    right_opm = (
        jnp.dot(standardized, latter_factor_matrix, preferred_element_type=jnp.float32)
        .astype(jnp.bfloat16)
        .reshape(count_seq, amino_shard_here, -1)
    )
    left_pair = jnp.dot(
        per_amino_features, row_amino_embedding, preferred_element_type=jnp.float32
    ).astype(jnp.bfloat16)
    right_pair = jnp.dot(
        per_amino_features, column_amino_embedding, preferred_element_type=jnp.float32
    ).astype(jnp.bfloat16)
    row_len = amino_collection // row_count
    col_len = amino_collection // col_count
    ratio = col_count // row_count
    row_a, row_b, row_left, row_right = (
        lax.all_gather(left_opm, "col", axis=1, tiled=True),
        lax.all_gather(right_opm, "col", axis=1, tiled=True),
        lax.all_gather(left_pair, "col", axis=0, tiled=True),
        lax.all_gather(right_pair, "col", axis=0, tiled=True),
    )
    offset = lax.axis_index("col") % ratio * col_len
    part_a = lax.dynamic_slice_in_dim(row_a, offset, col_len, 1)
    part_b = lax.dynamic_slice_in_dim(row_b, offset, col_len, 1)
    part_left = lax.dynamic_slice_in_dim(row_left, offset, col_len, 0)
    part_right = lax.dynamic_slice_in_dim(row_right, offset, col_len, 0)
    col_a, col_b, col_left, col_right = (
        spread_2(part_a, "row", lax.axis_index("col") // ratio),
        spread_2(part_b, "row", lax.axis_index("col") // ratio),
        spread_2(part_left, "row", lax.axis_index("col") // ratio),
        spread_2(part_right, "row", lax.axis_index("col") // ratio),
    )
    row_start = lax.axis_index("row") * row_len
    col_start = lax.axis_index("col") * col_len
    pair_output, logits = pair_block(
        row_a,
        col_b,
        row_left,
        col_right,
        row_start,
        col_start,
        offset_embedding_matrix,
        factor_mean_projection,
        grid_transition_expand,
        grid_transition_shrink,
        distance_bins_matrix,
    )
    ignored, mirror = pair_block(
        col_a,
        row_b,
        col_left,
        row_right,
        col_start,
        row_start,
        offset_embedding_matrix,
        factor_mean_projection,
        grid_transition_expand,
        grid_transition_shrink,
        distance_bins_matrix,
    )
    distogram = (logits + mirror.transpose(1, 0, 2)).astype(jnp.bfloat16)
    return (alignment_output, pair_output, distogram)


def solution(mesh):
    placed = (
        P(("row", "col"), None, None),
        P(("row", "col"), None),
        P(),
        P(),
        P(),
        P(),
        P(),
        P(),
        P(),
        P(),
        P(),
        P(),
        P(),
        P(),
        P(),
        P(),
        P(),
        P(),
    )
    return jax.shard_map(
        shards,
        mesh=mesh,
        in_specs=placed,
        out_specs=(P(None, ("row", "col"), None), P("row", "col", None), P("row", "col", None)),
        check_vma=False,
    )
```

profile of v0, /device:TPU:0, one launch (start us, length us, event | category | flops | bytes accessed | tf_op | source)
XLA Modules:
  0.0 171.2 jit_solution(15490688881708692075)
XLA Ops:
  7.2 1.2 copy.60
  8.4 0.8 copy.61
  9.2 7.3 %all-to-all-start = ((bf16[1,4,32,4,256]{4,3,1,0,2:T(4,128)(2,1)}), bf16[1,4,32,4,256]{4,3,1,0,2:T(4,128)(2,1)S(1)}, u32[]{:S(2)}, u32[]{:S(2)}) async-start(bf16[1,4,32,4,256]{4,3,1,0,2:T(4,128)(2,1)} %copy.61), calls=%async_computation | async-start | bytes 524288 | tf_op jit(solution)/shard_map/all_to_all | solution.py:172
  16.6 1.0 fusion.21
  17.6 12.0 %all-gather = bf16[8,4,128]{2,1,0:T(4,128)(2,1)S(1)} all-gather(bf16[1,4,128]{2,1,0:T(4,128)(2,1)S(1)} %fusion.21), channel_id=1, replica_groups=mesh['row'=4,'col'=8] {'col'}, dimensions={0}, use_global_device_ids=true | all-gather | bytes 9216 | tf_op jit(solution)/shard_map/all_gather | solution.py:213
  29.6 1.0 fusion.22
  30.6 8.9 %all-gather.1 = bf16[8,4,128]{2,1,0:T(4,128)(2,1)S(1)} all-gather(bf16[1,4,128]{2,1,0:T(4,128)(2,1)S(1)} %fusion.22), channel_id=1, replica_groups=mesh['row'=4,'col'=8] {'col'}, dimensions={0}, use_global_device_ids=true | all-gather | bytes 9216 | tf_op jit(solution)/shard_map/all_gather | solution.py:214
  39.6 10.2 %all-reduce = (bf16[16,128]{1,0:T(8,128)(2,1)S(1)}, bf16[16,128]{1,0:T(8,128)(2,1)S(1)}) all-reduce(bf16[16,128]{1,0:T(8,128)(2,1)S(1)} %dynamic-slice_select_fusion.1, bf16[16,128]{1,0:T(8,128)(2,1)S(1)} %dynamic-slice_select_fusion), channel_id=1, replica_groups=mesh['row'=4,'col'=8] {'row'}, use_global_device_ids=true, to_apply=%region_6.7 | all-reduce | flops 4096 | bytes 16384 | tf_op jit(solution)/shard_map/psum | solution.py:14
  50.3 0.7 broadcast_add_fusion
  51.4 0.5 multiply_reduce_fusion.3
  53.9 2.1 %fusion.24 = f32[4,8,128,128]{2,3,1,0:T(8,128)} fusion(bf16[128,4,8,32]{3,2,1,0:T(8,128)(2,1)S(1)} %reshape.300, bf16[128,4,8,32]{3,2,1,0:T(8,128)(2,1)S(1)} %reshape.299), kind=kOutput, calls=%fused_computation.44 | convolution fusion | flops 33554432 | bytes 2621440 | tf_op jit(solution)/shard_map/sihd,tihd->ihst/dot_general | solution.py:52
  56.1 1.2 fusion.72
  58.1 3.3 %convolution_bitcast_fusion = f32[128,4,8,32]{0,3,2,1:T(8,128)} fusion(bf16[128,4,8,32]{3,2,1,0:T(8,128)(2,1)S(1)} %reshape.298, f32[4,8,128]{2,1,0:T(8,128)S(1)} %fusion.72, f32[4,8,128,128]{2,3,1,0:T(8,128)} %fusion.24), kind=kOutput, calls=%fused_computation.16 | convolution fusion | flops 35655808 | bytes 2899968 | tf_op jit(solution)/shard_map/ihst,tihd->sihd/dot_general | solution.py:56
  61.4 2.9 %copy.66 = f32[128,4,8,32]{3,2,1,0:T(8,128)S(1)} copy(f32[128,4,8,32]{0,3,2,1:T(8,128)} %convolution_bitcast_fusion) | data formatting | bytes 1048576 | tf_op jit(solution)/shard_map/ihst,tihd->sihd/transpose | solution.py:56
  64.3 1.4 reshape.301
  65.7 1.6 fusion.77
  67.7 0.9 fusion.78
  69.5 14.4 %all_gather.14 = bf16[128,32,32]{0,2,1:T(8,128)(2,1)S(1)} all-gather(bf16[128,4,32]{0,2,1:T(8,128)(2,1)S(1)} %copy.68), channel_id=1, replica_groups=mesh['row'=4,'col'=8] {'col'}, dimensions={1}, use_global_device_ids=true | all-gather | bytes 294912 | tf_op jit(solution)/shard_map/all_gather | solution.py:211
  83.9 0.7 select_bitcast_fusion
  85.0 14.2 %all_gather.15 = bf16[128,32,32]{0,2,1:T(8,128)(2,1)S(1)} all-gather(bf16[128,4,32]{0,2,1:T(8,128)(2,1)S(1)} %copy.70), channel_id=1, replica_groups=mesh['row'=4,'col'=8] {'col'}, dimensions={1}, use_global_device_ids=true | all-gather | bytes 294912 | tf_op jit(solution)/shard_map/all_gather | solution.py:212
  99.2 0.7 select_bitcast_fusion.1
  100.1 0.8 convert_element_type.150
  100.9 39.5 %all-reduce.4.cloned.1.call-done = (bf16[16,32,128]{2,1,0:T(8,128)(2,1)}, bf16[16,32,128]{2,1,0:T(8,128)(2,1)}) async-done(((bf16[16,32,128]{2,1,0:T(8,128)(2,1)}, bf16[16,32,128]{2,1,0:T(8,128)(2,1)}), (bf16[16,32,128]{2,1,0:T(8,128)(2,1)}, bf16[16,32,128]{2,1,0:T(8,128)(2,1)})) %all-reduce.4.cloned.1.call-update) | async-done | bytes 262160 | tf_op jit(solution)/shard_map/psum | solution.py:14
  140.4 4.1 %fusion.2 = bf16[16,32,32,32]{3,2,1,0:T(8,128)(2,1)} fusion(bf16[128,32,32]{0,2,1:T(8,128)(2,1)S(1)} %all_gather.15, bf16[16,32,128]{2,1,0:T(8,128)(2,1)} %get-tuple-element.65), kind=kOutput, calls=%fused_computation.4 | convolution fusion | flops 135266304 | bytes 1441792 | tf_op jit(solution)/shard_map/while/body/eval_jaxpr/dot_general | solution.py:100
  144.5 6.2 %convert_element_type.168 = bf16[512,1024]{1,0:T(8,128)(2,1)S(1)} reshape(bf16[16,32,32,32]{3,2,1,0:T(8,128)(2,1)} %fusion.2) | data formatting | bytes 2097152 | tf_op jit(solution)/shard_map/while/body/eval_jaxpr/convert_element_type | solution.py:111
  150.7 0.5 fusion.83
  151.6 3.2 %fusion.1 = bf16[32,16,32,32]{3,2,1,0:T(8,128)(2,1)} fusion(bf16[128,32,32]{0,2,1:T(8,128)(2,1)S(1)} %all_gather.14, bf16[16,32,128]{2,1,0:T(8,128)(2,1)S(1)} %copy-done.6), kind=kOutput, calls=%fused_computation.3 | convolution fusion | flops 135266304 | bytes 1441792 | tf_op jit(solution)/shard_map/while/body/eval_jaxpr/dot_general | solution.py:100
  154.8 6.2 %convert_element_type.160 = bf16[512,1024]{1,0:T(8,128)(2,1)S(1)} reshape(bf16[32,16,32,32]{3,2,1,0:T(8,128)(2,1)} %fusion.1) | data formatting | bytes 2097152 | tf_op jit(solution)/shard_map/while/body/eval_jaxpr/convert_element_type | solution.py:111
  161.0 0.4 fusion.81
  162.1 0.6 fusion.19
  162.7 0.5 fusion.20
  163.6 0.8 fusion.34
  (93 shorter events, 6.9 us)
Async XLA Ops:
  7.2 60.5 %copy-start = (bf16[1024,256]{1,0:T(8,128)(2,1)S(1)}, bf16[1024,256]{1,0:T(8,128)(2,1)}, u32[]{:S(2)}) copy-start(bf16[1024,256]{1,0:T(8,128)(2,1)} %param.26) | copy-start | bytes 1572868
  9.2 43.2 %copy-start.3 = (bf16[256,256]{1,0:T(8,128)(2,1)S(1)}, bf16[256,256]{1,0:T(8,128)(2,1)}, u32[]{:S(2)}) copy-start(bf16[256,256]{1,0:T(8,128)(2,1)} %param.20) | copy-start | bytes 393220
  9.2 41.8 %all-to-all-start = ((bf16[1,4,32,4,256]{4,3,1,0,2:T(4,128)(2,1)}), bf16[1,4,32,4,256]{4,3,1,0,2:T(4,128)(2,1)S(1)}, u32[]{:S(2)}, u32[]{:S(2)}) async-start(bf16[1,4,32,4,256]{4,3,1,0,2:T(4,128)(2,1)} %copy.61), calls=%async_computation | async-start | bytes 524288 | tf_op jit(solution)/shard_map/all_to_all | solution.py:172
  16.5 123.8 %all-reduce.4.cloned.1.call-start = ((), (), s32[]{:S(2)}) async-start(), calls=%async_computation.1 | async-start | bytes 524288 | tf_op jit(solution)/shard_map/psum | solution.py:14
  51.9 1.3 copy-start.4
  56.1 1.3 copy-start.5
  61.4 4.3 %copy-start.13 = (bf16[256,256]{1,0:T(8,128)(2,1)S(1)}, bf16[256,256]{1,0:T(8,128)(2,1)}, u32[]{:S(2)}) copy-start(bf16[256,256]{1,0:T(8,128)(2,1)} %param.24) | copy-start | bytes 393220
  61.4 4.3 %copy-start.14 = (bf16[256,256]{1,0:T(8,128)(2,1)S(1)}, bf16[256,256]{1,0:T(8,128)(2,1)}, u32[]{:S(2)}) copy-start(bf16[256,256]{1,0:T(8,128)(2,1)} %param.23) | copy-start | bytes 393220
  65.7 1.9 %copy-start.12 = (bf16[256,1024]{1,0:T(8,128)(2,1)S(1)}, bf16[256,1024]{1,0:T(8,128)(2,1)}, u32[]{:S(2)}) copy-start(bf16[256,1024]{1,0:T(8,128)(2,1)} %param.25) | copy-start | bytes 1572868
  67.6 1.4 copy-start.10
  68.6 16.0 %copy-start.11 = (bf16[256,32]{0,1:T(8,128)(2,1)S(1)}, bf16[256,32]{0,1:T(8,128)(2,1)}, u32[]{:S(2)}) copy-start(bf16[256,32]{0,1:T(8,128)(2,1)} %param.28) | copy-start | bytes 49156
  68.6 31.3 %copy-start.1 = (f32[16,32,128]{2,1,0:T(8,128)S(1)}, f32[16,32,128]{2,1,0:T(8,128)}, u32[]{:S(2)}) copy-start(f32[16,32,128]{2,1,0:T(8,128)} %broadcast_add_fusion) | copy-start | bytes 786436
  144.5 6.2 %copy-start.2 = (bf16[1024,128]{1,0:T(8,128)(2,1)S(1)}, bf16[1024,128]{1,0:T(8,128)(2,1)}, u32[]{:S(2)}) copy-start(bf16[1024,128]{1,0:T(8,128)(2,1)} %param.29) | copy-start | bytes 786436
  144.5 6.7 %copy-start.8 = (bf16[65,128]{1,0:T(8,128)(2,1)S(1)}, bf16[65,128]{1,0:T(8,128)(2,1)}, u32[]{:S(2)}) copy-start(bf16[65,128]{1,0:T(8,128)(2,1)} %param.32) | copy-start | bytes 49924
  150.7 0.9 copy-start.6
  161.0 1.1 copy-start.15
  161.0 1.1 copy-start.16
  161.0 2.2 %copy-start.9 = (bf16[128,64]{0,1:T(8,128)(2,1)S(1)}, bf16[128,64]{0,1:T(8,128)(2,1)}, u32[]{:S(2)}) copy-start(bf16[128,64]{0,1:T(8,128)(2,1)} %param.35) | copy-start | bytes 49156
  163.2 1.2 copy-start.7
Sparse Core Ops, SparseCore 0:
  100.0 40.2 all-reduce.3
where the time goes:
time: 172 us; the launch traced here: 171 us
  blocking collectives  59.7 us (35%)
  waiting for transfers between devices  39.5 us (23%)
  matrix products  22.8 us (13%)
  local copies, waits for them, and re-layouts  22.4 us (13%)
  between operations  14.6 us (8%)
  starting transfers between devices  7.37 us (4%)
  other arithmetic  4.9 us (3%)
    psum x1, waiting for transfers between devices, spread_2(): return lax.psum(block, axis)  39.5 us
    all_gather x1, blocking collectives, shards(): lax.all_gather(left_opm, 'col', axis=1, tiled=True)  14.4 us
    all_gather x1, blocking collectives, shards(): lax.all_gather(right_opm, 'col', axis=1, tiled=True)  14.2 us
    convert_element_type x2, local copies, waits for them, and re-layouts, one_block(): outer = (outer / count_seq).astype(jnp.bfloat16)  12.4 us
    all_gather x1, blocking collectives, shards(): lax.all_gather(left_pair, 'col', axis=0, tiled=True)  12 us
    psum x1, blocking collectives, spread_2(): return lax.psum(block, axis)  10.2 us
    all_gather x1, blocking collectives, shards(): lax.all_gather(right_pair, 'col', axis=0, tiled=True)  8.93 us
    all_to_all x1, starting transfers between devices, shards(): lax.all_to_all(fragment_collection, ('row', 'col'), split_axis=2, concat_...  7.33 us
  transfers between devices with their start and end apart: 2, of which 1 were waited for; matrix products, arithmetic and copies ran while one was open for 2% of the time, Pallas kernels for 0%

commit v1 on v0

--- a/solution.py
+++ b/solution.py
@@ -7,11 +7,12 @@
 HEADS = 8
 HEAD = 32
 CLIP = 32
+_produce_cube = lambda frame, lane_axis: jnp.sum(lax.all_gather(frame, lane_axis), axis=0)
 
 
 def spread_2(block, axis, source):
     block = jnp.where(lax.axis_index(axis) == source, block, jnp.zeros_like(block))
-    return lax.psum(block, axis)
+    return _produce_cube(block, axis)
 
 
 def standardize_features(values):

time: 172 us -> 154 us (0.90)
  waiting for transfers between devices: 39.5 us -> 0.01 us
  blocking collectives: 59.7 us -> 87.4 us
  between operations: 14.6 us -> 1.2 us
  local copies, waits for them, and re-layouts: 22.4 us -> 28.5 us
    psum x1 -> x0, waiting for transfers between devices: 39.5 us -> none  [spread_2(): return lax.psum(block, axis)]
    all_gather x0 -> x4, blocking collectives: none -> 36.7 us  [lax.all_gather(frame, lane_axis)]
    psum x1 -> x0, blocking collectives: 10.2 us -> none  [spread_2(): return lax.psum(block, axis)]
    all_gather x0 -> x2, local copies, waits for them, and re-layouts: none -> 3.95 us  [lax.all_gather(frame, lane_axis)]
    all_gather x1, blocking collectives: 8.93 us -> 12 us  [shards(): lax.all_gather(right_pair, 'col', axis=0, tiled=True)]
    all_gather x1, blocking collectives: 12 us -> 8.98 us  [shards(): lax.all_gather(left_pair, 'col', axis=0, tiled=True)]
  transfers between devices with their start and end apart: 2 -> 1, of which waited for: 1 -> 0; matrix products, arithmetic and copies ran while one was open for 2% -> 3% of each run, Pallas kernels for 0% -> 0%
where the time goes in v1:
time: 154 us; the launch traced here: 153 us
  blocking collectives  87.4 us (57%)
  local copies, waits for them, and re-layouts  28.5 us (19%)
  matrix products  22.9 us (15%)
  starting transfers between devices  7.33 us (5%)
  other arithmetic  6.06 us (4%)
    all_gather x4, blocking collectives, lax.all_gather(frame, lane_axis)  36.7 us
    all_gather x1, blocking collectives, shards(): lax.all_gather(left_opm, 'col', axis=1, tiled=True)  15.4 us
    all_gather x1, blocking collectives, shards(): lax.all_gather(right_opm, 'col', axis=1, tiled=True)  14.3 us
    convert_element_type x2, local copies, waits for them, and re-layouts, one_block(): outer = (outer / count_seq).astype(jnp.bfloat16)  12.4 us
    all_gather x1, blocking collectives, shards(): lax.all_gather(right_pair, 'col', axis=0, tiled=True)  12 us
    all_gather x1, blocking collectives, shards(): lax.all_gather(left_pair, 'col', axis=0, tiled=True)  8.98 us
    dot_general x2, matrix products, one_block(): lax.dot_general(a_blk.reshape(count_seq, step_rows * factor), flat_v, (((...  7.34 us
    all_to_all x1, starting transfers between devices, shards(): lax.all_to_all(fragment_collection, ('row', 'col'), split_axis=2, concat_...  7.33 us
  transfers between devices with their start and end apart: 1, of which 0 were waited for; matrix products, arithmetic and copies ran while one was open for 3% of the time, Pallas kernels for 0%

profile of v1, /device:TPU:0, one launch (start us, length us, event | category | flops | bytes accessed | tf_op | source)
XLA Modules:
  0.0 153.4 jit_solution(1609138964029612331)
XLA Ops:
  0.6 1.2 copy.61
  1.9 0.8 copy.62
  2.7 7.3 %all-to-all-start = ((bf16[1,4,32,4,256]{4,3,1,0,2:T(4,128)(2,1)}), bf16[1,4,32,4,256]{4,3,1,0,2:T(4,128)(2,1)S(1)}, u32[]{:S(2)}, u32[]{:S(2)}) async-start(bf16[1,4,32,4,256]{4,3,1,0,2:T(4,128)(2,1)} %copy.62), calls=%async_computation | async-start | bytes 524288 | tf_op jit(solution)/shard_map/all_to_all | solution.py:173
  10.0 1.0 fusion.22
  11.0 12.0 %all-gather.5 = bf16[8,4,128]{2,1,0:T(4,128)(2,1)S(1)} all-gather(bf16[1,4,128]{2,1,0:T(4,128)(2,1)S(1)} %fusion.22), channel_id=1, replica_groups=mesh['row'=4,'col'=8] {'col'}, dimensions={0}, use_global_device_ids=true | all-gather | bytes 9216 | tf_op jit(solution)/shard_map/all_gather | solution.py:215
  23.0 1.0 fusion.21
  24.0 9.0 %all-gather.4 = bf16[8,4,128]{2,1,0:T(4,128)(2,1)S(1)} all-gather(bf16[1,4,128]{2,1,0:T(4,128)(2,1)S(1)} %fusion.21), channel_id=1, replica_groups=mesh['row'=4,'col'=8] {'col'}, dimensions={0}, use_global_device_ids=true | all-gather | bytes 9216 | tf_op jit(solution)/shard_map/all_gather | solution.py:214
  33.3 8.3 %all-gather.2 = bf16[64,128]{1,0:T(8,128)(2,1)S(1)} all-gather(bf16[16,128]{1,0:T(8,128)(2,1)S(1)} %dynamic-slice_select_fusion.2), channel_id=4, replica_groups=mesh['row'=4,'col'=8] {'row'}, dimensions={0}, use_global_device_ids=true | all-gather | bytes 20480 | tf_op jit(solution)/shard_map/all_gather | solution.py:10
  41.7 8.1 %all-gather = bf16[64,128]{1,0:T(8,128)(2,1)S(1)} all-gather(bf16[16,128]{1,0:T(8,128)(2,1)S(1)} %dynamic-slice_select_fusion.3), channel_id=2, replica_groups=mesh['row'=4,'col'=8] {'row'}, dimensions={0}, use_global_device_ids=true | all-gather | bytes 20480 | tf_op jit(solution)/shard_map/all_gather | solution.py:10
  49.9 0.8 copy.75
  54.6 1.2 fusion.72
  55.8 2.1 %fusion.24 = f32[4,8,128,128]{2,3,1,0:T(8,128)} fusion(bf16[128,4,8,32]{3,2,1,0:T(8,128)(2,1)S(1)} %reshape.302, bf16[128,4,8,32]{3,2,1,0:T(8,128)(2,1)S(1)} %reshape.301), kind=kOutput, calls=%fused_computation.44 | convolution fusion | flops 33554432 | bytes 2621440 | tf_op jit(solution)/shard_map/sihd,tihd->ihst/dot_general | solution.py:53
  58.8 3.3 %convolution_bitcast_fusion = f32[128,4,8,32]{0,3,2,1:T(8,128)} fusion(bf16[128,4,8,32]{3,2,1,0:T(8,128)(2,1)S(1)} %reshape.300, f32[4,8,128]{2,1,0:T(8,128)S(1)} %fusion.72, f32[4,8,128,128]{2,3,1,0:T(8,128)} %fusion.24), kind=kOutput, calls=%fused_computation.16 | convolution fusion | flops 35655808 | bytes 2899968 | tf_op jit(solution)/shard_map/ihst,tihd->sihd/dot_general | solution.py:57
  62.1 2.9 %copy.67 = f32[128,4,8,32]{3,2,1,0:T(8,128)S(1)} copy(f32[128,4,8,32]{0,3,2,1:T(8,128)} %convolution_bitcast_fusion) | data formatting | bytes 1048576 | tf_op jit(solution)/shard_map/ihst,tihd->sihd/transpose | solution.py:57
  65.0 1.4 reshape.303
  66.4 1.6 %fusion.77 = (f32[512]{0:T(512)S(1)}, f32[512,256]{1,0:T(8,128)S(1)}) fusion(f32[512,256]{1,0:T(8,128)S(1)} %reshape.313, bf16[256,256]{1,0:T(8,128)(2,1)S(1)} %copy-done.16, f32[512,256]{1,0:T(8,128)} %reshape.303, bf16[256,256]{1,0:T(8,128)(2,1)S(1)} %copy-done.17, f32[512]{0:T(512)S(1)} %rsqrt.46, f32[512]{0:T(512)S(1)} %div.73), kind=kOutput, calls=%fused_computation.109 | convolution fusion | flops 135527936 | bytes 1841152 | tf_op jit(solution)/shard_map/dot_general | solution.py:61
  68.3 0.9 fusion.78
  69.7 0.8 convert_element_type.164
  70.9 15.4 %all_gather.40 = bf16[128,32,32]{0,2,1:T(8,128)(2,1)} all-gather(bf16[128,4,32]{0,2,1:T(8,128)(2,1)S(1)} %copy.69), channel_id=1, replica_groups=mesh['row'=4,'col'=8] {'col'}, dimensions={1}, use_global_device_ids=true | all-gather | bytes 294912 | tf_op jit(solution)/shard_map/all_gather | solution.py:212
  86.8 14.3 %all_gather.41 = bf16[128,32,32]{0,2,1:T(8,128)(2,1)S(1)} all-gather(bf16[128,4,32]{0,2,1:T(8,128)(2,1)S(1)} %copy.71), channel_id=1, replica_groups=mesh['row'=4,'col'=8] {'col'}, dimensions={1}, use_global_device_ids=true | all-gather | bytes 294912 | tf_op jit(solution)/shard_map/all_gather | solution.py:213
  101.1 9.3 %all-gather.1 = bf16[512,16,32]{0,2,1:T(8,128)(2,1)S(1)} all-gather(bf16[128,16,32]{0,2,1:T(8,128)(2,1)S(1)} %dynamic-slice_select_fusion.1), channel_id=3, replica_groups=mesh['row'=4,'col'=8] {'row'}, dimensions={0}, use_global_device_ids=true | all-gather | bytes 655360 | tf_op jit(solution)/shard_map/all_gather | solution.py:10
  110.4 2.0 %copy.87 = bf16[512,16,32]{2,1,0:T(8,128)(2,1)S(1)} copy(bf16[512,16,32]{0,2,1:T(8,128)(2,1)S(1)} %all-gather.1) | data formatting | bytes 1048576 | tf_op jit(solution)/shard_map/all_gather | solution.py:10
  112.4 0.8 reduce_sum.159
  113.6 0.9 dynamic-slice_select_fusion
  114.6 4.1 %fusion.1 = bf16[32,16,32,32]{3,2,1,0:T(8,128)(2,1)} fusion(bf16[128,32,32]{0,2,1:T(8,128)(2,1)} %all_gather.40, bf16[128,16,32]{0,2,1:T(8,128)(2,1)S(1)} %copy.73), kind=kOutput, calls=%fused_computation.3 | convolution fusion | flops 135266304 | bytes 1441792 | tf_op jit(solution)/shard_map/while/body/eval_jaxpr/dot_general | solution.py:101
  118.7 6.2 %convert_element_type.174 = bf16[512,1024]{1,0:T(8,128)(2,1)S(1)} reshape(bf16[32,16,32,32]{3,2,1,0:T(8,128)(2,1)} %fusion.1) | data formatting | bytes 2097152 | tf_op jit(solution)/shard_map/while/body/eval_jaxpr/convert_element_type | solution.py:112
  126.5 10.9 %all-gather.3 = bf16[512,16,32]{0,2,1:T(8,128)(2,1)S(1)} all-gather(bf16[128,16,32]{0,2,1:T(8,128)(2,1)S(1)} %dynamic-slice_select_fusion), channel_id=5, replica_groups=mesh['row'=4,'col'=8] {'row'}, dimensions={0}, use_global_device_ids=true | all-gather | bytes 655360 | tf_op jit(solution)/shard_map/all_gather | solution.py:10
  137.4 2.0 %copy.88 = bf16[512,16,32]{2,1,0:T(8,128)(2,1)S(1)} copy(bf16[512,16,32]{0,2,1:T(8,128)(2,1)S(1)} %all-gather.3) | data formatting | bytes 1048576 | tf_op jit(solution)/shard_map/all_gather | solution.py:10
  139.4 0.8 reduce_sum.163
  140.7 3.2 %fusion.2 = bf16[16,32,32,32]{3,2,1,0:T(8,128)(2,1)} fusion(bf16[128,32,32]{0,2,1:T(8,128)(2,1)S(1)} %all_gather.41, bf16[128,16,32]{0,2,1:T(8,128)(2,1)S(1)} %copy.77), kind=kOutput, calls=%fused_computation.4 | convolution fusion | flops 135266304 | bytes 1441792 | tf_op jit(solution)/shard_map/while/body/eval_jaxpr/dot_general | solution.py:101
  143.9 6.2 %convert_element_type.182 = bf16[512,1024]{1,0:T(8,128)(2,1)S(1)} reshape(bf16[16,32,32,32]{3,2,1,0:T(8,128)(2,1)} %fusion.2) | data formatting | bytes 2097152 | tf_op jit(solution)/shard_map/while/body/eval_jaxpr/convert_element_type | solution.py:112
  152.6 0.8 fusion.34
  (107 shorter events, 11.3 us)
Async XLA Ops:
  0.6 67.7 %copy-start = (bf16[1024,256]{1,0:T(8,128)(2,1)S(1)}, bf16[1024,256]{1,0:T(8,128)(2,1)}, u32[]{:S(2)}) copy-start(bf16[1024,256]{1,0:T(8,128)(2,1)} %param.26) | copy-start | bytes 1572868
  2.7 49.0 %all-to-all-start = ((bf16[1,4,32,4,256]{4,3,1,0,2:T(4,128)(2,1)}), bf16[1,4,32,4,256]{4,3,1,0,2:T(4,128)(2,1)S(1)}, u32[]{:S(2)}, u32[]{:S(2)}) async-start(bf16[1,4,32,4,256]{4,3,1,0,2:T(4,128)(2,1)} %copy.62), calls=%async_computation | async-start | bytes 524288 | tf_op jit(solution)/shard_map/all_to_all | solution.py:173
  41.6 11.4 %copy-start.7 = (bf16[256,256]{1,0:T(8,128)(2,1)S(1)}, bf16[256,256]{1,0:T(8,128)(2,1)}, u32[]{:S(2)}) copy-start(bf16[256,256]{1,0:T(8,128)(2,1)} %param.21) | copy-start | bytes 393220
  51.8 2.0 %copy-start.8 = (bf16[256,256]{1,0:T(8,128)(2,1)S(1)}, bf16[256,256]{1,0:T(8,128)(2,1)}, u32[]{:S(2)}) copy-start(bf16[256,256]{1,0:T(8,128)(2,1)} %param.20) | copy-start | bytes 393220
  55.8 2.1 %copy-start.9 = (bf16[256,256]{1,0:T(8,128)(2,1)S(1)}, bf16[256,256]{1,0:T(8,128)(2,1)}, u32[]{:S(2)}) copy-start(bf16[256,256]{1,0:T(8,128)(2,1)} %param.22) | copy-start | bytes 393220
  62.1 4.3 %copy-start.16 = (bf16[256,256]{1,0:T(8,128)(2,1)S(1)}, bf16[256,256]{1,0:T(8,128)(2,1)}, u32[]{:S(2)}) copy-start(bf16[256,256]{1,0:T(8,128)(2,1)} %param.24) | copy-start | bytes 393220
  62.1 4.3 %copy-start.17 = (bf16[256,256]{1,0:T(8,128)(2,1)S(1)}, bf16[256,256]{1,0:T(8,128)(2,1)}, u32[]{:S(2)}) copy-start(bf16[256,256]{1,0:T(8,128)(2,1)} %param.23) | copy-start | bytes 393220
  66.4 1.9 %copy-start.15 = (bf16[256,1024]{1,0:T(8,128)(2,1)S(1)}, bf16[256,1024]{1,0:T(8,128)(2,1)}, u32[]{:S(2)}) copy-start(bf16[256,1024]{1,0:T(8,128)(2,1)} %param.25) | copy-start | bytes 1572868
  68.3 2.2 %copy-start.13 = (bf16[256,32]{0,1:T(8,128)(2,1)S(1)}, bf16[256,32]{0,1:T(8,128)(2,1)}, u32[]{:S(2)}) copy-start(bf16[256,32]{0,1:T(8,128)(2,1)} %param.27) | copy-start | bytes 49156
  69.3 17.1 %copy-start.14 = (bf16[256,32]{0,1:T(8,128)(2,1)S(1)}, bf16[256,32]{0,1:T(8,128)(2,1)}, u32[]{:S(2)}) copy-start(bf16[256,32]{0,1:T(8,128)(2,1)} %param.28) | copy-start | bytes 49156
  118.7 6.2 %copy-start.5 = (bf16[1024,128]{1,0:T(8,128)(2,1)S(1)}, bf16[1024,128]{1,0:T(8,128)(2,1)}, u32[]{:S(2)}) copy-start(bf16[1024,128]{1,0:T(8,128)(2,1)} %param.29) | copy-start | bytes 786436
  118.7 6.7 %copy-start.2 = (f32[32,16,128]{2,1,0:T(8,128)S(1)}, f32[32,16,128]{2,1,0:T(8,128)}, u32[]{:S(2)}) copy-start(f32[32,16,128]{2,1,0:T(8,128)} %broadcast_add_fusion.1) | copy-start | bytes 786436
  118.7 6.7 %copy-start.11 = (bf16[65,128]{1,0:T(8,128)(2,1)S(1)}, bf16[65,128]{1,0:T(8,128)(2,1)}, u32[]{:S(2)}) copy-start(bf16[65,128]{1,0:T(8,128)(2,1)} %param.32) | copy-start | bytes 49924
  125.8 0.7 copy-start.3
  143.8 6.2 %copy-start.6 = (bf16[1024,128]{1,0:T(8,128)(2,1)S(1)}, bf16[1024,128]{1,0:T(8,128)(2,1)}, u32[]{:S(2)}) copy-start(bf16[1024,128]{1,0:T(8,128)(2,1)} %param.29) | copy-start | bytes 786436
  143.8 6.8 %copy-start.1 = (f32[512,128]{0,1:T(8,128)S(1)}, f32[512,128]{0,1:T(8,128)}, u32[]{:S(2)}) copy-start(f32[512,128]{0,1:T(8,128)} %copy.75) | copy-start | bytes 786436
  150.1 1.0 copy-start.4
  150.1 1.0 copy-start.18
  150.1 1.0 copy-start.19
  150.1 2.1 %copy-start.12 = (bf16[128,64]{0,1:T(8,128)(2,1)S(1)}, bf16[128,64]{0,1:T(8,128)(2,1)}, u32[]{:S(2)}) copy-start(bf16[128,64]{0,1:T(8,128)(2,1)} %param.35) | copy-start | bytes 49156
  151.6 1.8 %copy-start.10 = (bf16[512,128]{1,0:T(8,128)(2,1)}, bf16[512,128]{1,0:T(8,128)(2,1)S(1)}, u32[]{:S(2)}) copy-start(bf16[512,128]{1,0:T(8,128)(2,1)S(1)} %fusion.20) | copy-start | bytes 393220
